TPU v7x, 32 devices: a whole 2x2x4 slice. The times are simulated.
32 devices in a mesh: dom: 8 (over z, y), sub: 4 (over x, core).
Axes of the slice: x: 2, y: 2, z: 4, core: 2. Of those that a mesh axis runs over, the one named last changes fastest.
Arguments:
- nodes: bfloat16 [16384, 128], P(('dom', 'sub')), may hold values from -6 to 6
- edges: bfloat16 [65536, 128], P(('dom', 'sub')), may hold values from -6 to 6
- senders: int32 [65536], P(('dom', 'sub')), may hold values from 0 to 895
- receivers: int32 [65536], P(('dom', 'sub')), may hold values from 0 to 511
- edge_live: int32 [65536], P(('dom', 'sub')), may hold values from 0 to 1, as said below
- outlet_flags: int32 [16384], P(('dom', 'sub')), may hold values 0 or 1
- send_rows: int32 [12288], P(('dom', 'sub')), may hold values from 0 to 511
- edge_first: float32 [3, 384, 128], replicated, may hold values from -0.3125 to 0.3125
- edge_bias: float32 [3, 128], replicated, may hold values from -3 to 3
- edge_second: float32 [3, 128, 128], replicated, may hold values from -0.5 to 0.5
- edge_offset: float32 [3, 128], replicated, may hold values from -3 to 3
- edge_gain: float32 [3, 128], replicated, may hold values from 0.25 to 1.75
- node_first: float32 [3, 256, 128], replicated, may hold values from -0.375 to 0.375
- node_bias: float32 [3, 128], replicated, may hold values from -3 to 3
- node_second: float32 [3, 128, 128], replicated, may hold values from -0.5 to 0.5
- node_offset: float32 [3, 128], replicated, may hold values from -3 to 3
- node_gain: float32 [3, 128], replicated, may hold values from 0.25 to 1.75
- outlet_map: float32 [3, 128, 128], replicated, may hold values from -0.5 to 0.5
- grad_out: float32 [16384, 128], P(('dom', 'sub')), may hold values from -6 to 6
Outputs:
- latent_out: float32 [16384, 128], P(('dom', 'sub'))
- latent_grad: float32 [16384, 128], P(('dom', 'sub'))
- edge_first_grad: float32 [3, 384, 128], replicated
- edge_bias_grad: float32 [3, 128], replicated
- edge_second_grad: float32 [3, 128, 128], replicated
- edge_offset_grad: float32 [3, 128], replicated
- edge_gain_grad: float32 [3, 128], replicated
- node_first_grad: float32 [3, 256, 128], replicated
- node_bias_grad: float32 [3, 128], replicated
- node_second_grad: float32 [3, 128, 128], replicated
- node_offset_grad: float32 [3, 128], replicated
- node_gain_grad: float32 [3, 128], replicated
- outlet_map_grad: float32 [3, 128, 128], replicated
Inputs may be any that keep to these rules, and one draw needn't show every extreme that they name: `edge_live`: on each device the live edge slots are the first ones of its 2048; each device has between a quarter and all of them live, and some device has all live. `senders`: indices below 512 name the device's own nodes; higher ones name halo rows.
All inputs are finite; a program needn't handle non-finite values. No bound on the sum of `outlet_flags` on one device may be relied on, other than what follows from the above.
Results may differ from a plain program's by a relative error of at most 0.018.
Values may be sent and summed in bfloat16 or wider, within the bound.
A program may use at most 320 MiB of HBM per device.

v0:
```python
import jax
import jax.numpy as jnp
from jax import lax
from jax.sharding import PartitionSpec as P


def passed_along(value, axis, steps):
    count = lax.axis_size(axis)
    first, last = (max(0, -steps), min(count, count - steps))
    return lax.ppermute(value, axis, [(source, source + steps) for source in range(first, last)])


def normalize(values):
    mean = jnp.mean(values, axis=-1, keepdims=True)
    centered = values - mean
    variance = jnp.mean(centered * centered, axis=-1, keepdims=True)
    return centered * lax.rsqrt(variance + 1e-05)


def layer_local(latent, edge_state, halo, layer_weights, senders, receivers, live, flags):
    (
        edge_first,
        edge_bias,
        edge_second,
        edge_offset,
        edge_gain,
        node_first,
        node_bias,
        node_second,
        node_offset,
        node_gain,
        outlet_map,
    ) = layer_weights
    own = latent.astype(jnp.bfloat16)
    extended = jnp.concatenate([own, halo], axis=0)
    joined = jnp.concatenate(
        [edge_state.astype(jnp.bfloat16), extended[senders], own[receivers]], axis=1
    )
    act_one = jax.nn.silu(
        jnp.dot(joined, edge_first.astype(jnp.bfloat16), preferred_element_type=jnp.float32)
        + edge_bias
    ).astype(jnp.bfloat16)
    pre_two = (
        jnp.dot(act_one, edge_second.astype(jnp.bfloat16), preferred_element_type=jnp.float32)
        + edge_offset
    )
    message = live[:, None] * (edge_gain * normalize(pre_two))
    new_edge = edge_state + message
    summed = jax.ops.segment_sum(message, receivers, num_segments=latent.shape[0])
    summed_half = summed.astype(jnp.bfloat16)
    node_in = jnp.concatenate([own, summed_half], axis=1)
    node_hidden = jax.nn.silu(
        jnp.dot(node_in, node_first.astype(jnp.bfloat16), preferred_element_type=jnp.float32)
        + node_bias
    ).astype(jnp.bfloat16)
    update = node_gain * normalize(
        jnp.dot(node_hidden, node_second.astype(jnp.bfloat16), preferred_element_type=jnp.float32)
        + node_offset
    )
    outlet = flags[:, None] * jnp.dot(
        summed_half, outlet_map.astype(jnp.bfloat16), preferred_element_type=jnp.float32
    )
    return (latent + update + outlet, new_edge)


def send_halo(latent, send_rows, low, high):
    sent = latent[send_rows].astype(jnp.bfloat16)
    from_lower = passed_along(sent[low : 2 * low], "sub", 1)
    from_upper = passed_along(sent[:low], "sub", -1)
    dom_lower = passed_along(sent[2 * low + high :], "dom", 1)
    dom_upper = passed_along(sent[2 * low : 2 * low + high], "dom", -1)
    return jnp.concatenate([from_lower, from_upper, dom_lower, dom_upper], axis=0)


def return_halo(halo_grad, send_rows, low, high, shape):
    back_high = passed_along(halo_grad[:low], "sub", -1)
    back_low = passed_along(halo_grad[low : 2 * low], "sub", 1)
    dom_back_high = passed_along(halo_grad[2 * low : 2 * low + high], "dom", -1)
    dom_back_low = passed_along(halo_grad[2 * low + high :], "dom", 1)
    returned = jnp.concatenate([back_low, back_high, dom_back_low, dom_back_high], axis=0).astype(
        jnp.float32
    )
    return jnp.zeros(shape, jnp.float32).at[send_rows].add(returned)


def flatten_all(grads):
    return jnp.concatenate([grad.reshape(-1) for grad in grads])


def unflatten_all(flat, shapes):
    pieces = []
    offset = 0
    for shape in shapes:
        length = 1
        for extent in shape:
            length = length * extent
        pieces.append(flat[offset : offset + length].reshape(shape))
        offset = offset + length
    return pieces


def on_device(
    nodes,
    edges,
    senders,
    receivers,
    edge_live,
    outlet_flags,
    send_rows,
    edge_first,
    edge_bias,
    edge_second,
    edge_offset,
    edge_gain,
    node_first,
    node_bias,
    node_second,
    node_offset,
    node_gain,
    outlet_map,
    grad_out,
):
    weights = (
        edge_first,
        edge_bias,
        edge_second,
        edge_offset,
        edge_gain,
        node_first,
        node_bias,
        node_second,
        node_offset,
        node_gain,
        outlet_map,
    )
    layers = edge_first.shape[0]
    low = nodes.shape[0] // 8
    high = nodes.shape[0] // 4
    live = edge_live.astype(jnp.float32)
    flags = outlet_flags.astype(jnp.float32)
    latent = nodes.astype(jnp.float32)
    edge_state = edges.astype(jnp.float32)

    def advance(latent_in, edge_in, halo, layer_weights):
        return layer_local(latent_in, edge_in, halo, layer_weights, senders, receivers, live, flags)

    saved = []
    for layer in range(layers):
        layer_weights = tuple((weight[layer] for weight in weights))
        halo = send_halo(latent, send_rows, low, high)
        (latent, edge_state), pullback = jax.vjp(advance, latent, edge_state, halo, layer_weights)
        saved.append(pullback)
    layer_shapes = [weight.shape[1:] for weight in weights]
    latent_grad = grad_out
    edge_grad = jnp.zeros_like(edge_state)
    per_layer = [None] * layers
    for layer in reversed(range(layers)):
        pullback = saved[layer]
        latent_grad, edge_grad, halo_grad, weight_grads = pullback((latent_grad, edge_grad))
        latent_grad = latent_grad + return_halo(halo_grad, send_rows, low, high, latent_grad.shape)
        flat = flatten_all(weight_grads)
        per_layer[layer] = flat
    stacked = jnp.stack(per_layer, axis=0)
    stacked = lax.psum(stacked, ("dom", "sub"))
    by_layer = [unflatten_all(stacked[layer], layer_shapes) for layer in range(layers)]
    results = [
        jnp.stack([by_layer[layer][which] for layer in range(layers)], axis=0)
        for which in range(len(weights))
    ]
    return (
        latent,
        latent_grad,
        results[0],
        results[1],
        results[2],
        results[3],
        results[4],
        results[5],
        results[6],
        results[7],
        results[8],
        results[9],
        results[10],
    )


def solution(mesh):
    placed = (
        P(("dom", "sub"), None),
        P(("dom", "sub"), None),
        P(("dom", "sub")),
        P(("dom", "sub")),
        P(("dom", "sub")),
        P(("dom", "sub")),
        P(("dom", "sub")),
        P(),
        P(),
        P(),
        P(),
        P(),
        P(),
        P(),
        P(),
        P(),
        P(),
        P(),
        P(("dom", "sub"), None),
    )
    return jax.shard_map(
        on_device,
        mesh=mesh,
        in_specs=placed,
        out_specs=(
            P(("dom", "sub"), None),
            P(("dom", "sub"), None),
            P(),
            P(),
            P(),
            P(),
            P(),
            P(),
            P(),
            P(),
            P(),
            P(),
            P(),
        ),
        check_vma=False,
    )
```

profile of v0, /device:TPU:0, one launch (start us, length us, event | category | flops | bytes accessed | tf_op | source)
XLA Modules:
  0.0 548.7 jit_solution(7893833300528265434)
XLA Ops:
  12.7 3.8 collective-permute-start
  18.4 6.1 %collective-permute-start.2 = (bf16[128,128]{1,0:T(8,128)(2,1)}, bf16[128,128]{1,0:T(8,128)(2,1)}, u32[]{:S(2)}, u32[]{:S(2)}) collective-permute-start(bf16[128,128]{1,0:T(8,128)(2,1)} %get-tuple-element.114), channel_id=1, source_target_pairs={{0,4},{4,8},{8,12},{12,16},{16,20},{20,24},{24,28},{1,5},{5,9},{9,... | collective-permute-start | bytes 98312 | tf_op jit(solution)/shard_map/ppermute | solution.py:10
  33.6 6.2 %gather_fusion.2 = bf16[2048,128]{1,0:T(8,128)(2,1)S(1)} fusion(bf16[512,128]{1,0:T(8,128)(2,1)S(1)} %copy-done, s32[2048]{0:T(1024)S(1)} %get-tuple-element.118), kind=kCustom, calls=%fused_computation.2 | custom fusion | bytes 1056768 | tf_op jit(solution)/shard_map/jvp()/gather | solution.py:37
  42.0 6.2 %gather_fusion.1 = bf16[2048,128]{1,0:T(8,128)(2,1)S(1)} fusion(bf16[896,128]{1,0:T(8,128)(2,1)S(1)} %constant_dynamic-update-slice_fusion, s32[2048]{0:T(1024)S(1)} %get-tuple-element.121), kind=kCustom, calls=%fused_computation.1 | custom fusion | bytes 1056768 | tf_op jit(solution)/shard_map/jvp()/gather | solution.py:37
  53.7 11.9 %scatter_custom_fusion = f32[512,128]{1,0:T(8,128)S(1)} fusion(s32[2048]{0:T(1024)S(1)} %copy-done.84, f32[2048,128]{1,0:T(8,128)} %copy.74, f32[]{:T(128)} %constant.51.clone.1), kind=kCustom, calls=%fused_computation.256 | custom fusion | flops 262144 | bytes 262656 | tf_op jit(solution)/shard_map/jvp()/scatter-add | solution.py:49
  71.2 5.5 collective-permute-start.6
  78.6 3.2 collective-permute-start.4
  82.0 6.2 %gather_fusion.5 = bf16[2048,128]{1,0:T(8,128)(2,1)S(1)} fusion(bf16[512,128]{1,0:T(8,128)(2,1)S(1)} %copy.80, s32[2048]{0:T(1024)S(1)} %copy-done.66), kind=kCustom, calls=%fused_computation.5 | custom fusion | bytes 1056768 | tf_op jit(solution)/shard_map/jvp()/gather | solution.py:37
  91.0 6.2 %gather_fusion.4 = bf16[2048,128]{1,0:T(8,128)(2,1)S(1)} fusion(bf16[896,128]{1,0:T(8,128)(2,1)S(1)} %copy.79, s32[2048]{0:T(1024)S(1)} %copy-done.60), kind=kCustom, calls=%fused_computation.4 | custom fusion | bytes 1056768 | tf_op jit(solution)/shard_map/jvp()/gather | solution.py:37
  98.2 2.0 convolution_add_fusion.3
  104.0 2.6 copy.83
  106.6 11.9 %scatter_custom_fusion.1 = f32[512,128]{1,0:T(8,128)S(1)} fusion(s32[2048]{0:T(1024)S(1)} %copy-done.85, f32[2048,128]{1,0:T(8,128)} %copy.83, f32[]{:T(128)} %constant.51.clone.1), kind=kCustom, calls=%fused_computation.254 | custom fusion | flops 262144 | bytes 262656 | tf_op jit(solution)/shard_map/jvp()/scatter-add | solution.py:49
  126.5 4.4 collective-permute-start.8
  132.2 5.3 collective-permute-start.10
  137.7 7.2 %gather_fusion.8 = bf16[2048,128]{1,0:T(8,128)(2,1)S(1)} fusion(bf16[512,128]{1,0:T(8,128)(2,1)S(1)} %copy.89, s32[2048]{0:T(1024)} %copy-done.65), kind=kCustom, calls=%fused_computation.8 | custom fusion | bytes 1056768 | tf_op jit(solution)/shard_map/jvp()/gather | solution.py:37
  147.1 7.2 %gather_fusion.7 = bf16[2048,128]{1,0:T(8,128)(2,1)S(1)} fusion(bf16[896,128]{1,0:T(8,128)(2,1)S(1)} %copy.88, s32[2048]{0:T(1024)} %copy-done.59), kind=kCustom, calls=%fused_computation.7 | custom fusion | bytes 1056768 | tf_op jit(solution)/shard_map/jvp()/gather | solution.py:37
  155.2 2.0 convolution_add_fusion.1
  161.1 2.5 copy.92
  163.6 12.9 %scatter_custom_fusion.2 = f32[512,128]{1,0:T(8,128)} fusion(s32[2048]{0:T(1024)} %param.22, f32[2048,128]{1,0:T(8,128)} %copy.92, f32[]{:T(128)} %constant.51.clone.1), kind=kCustom, calls=%fused_computation.252 | custom fusion | flops 262144 | bytes 262656 | tf_op jit(solution)/shard_map/jvp()/scatter-add | solution.py:49
  176.5 1.7 copy.93
  178.2 1.8 fusion.37
  185.7 1.7 fusion.192
  190.0 8.4 %gather_fusion.9 = f32[2048,128]{1,0:T(8,128)} fusion(f32[512,128]{1,0:T(8,128)S(1)} %fusion.19, s32[2048]{0:T(1024)} %get-tuple-element.119), kind=kCustom, calls=%fused_computation.9 | custom fusion | bytes 2105344 | tf_op jit(solution)/shard_map/transpose(jvp())/gather | solution.py:49
  198.3 2.6 copy.97
  200.9 2.2 multiply_reduce_fusion
  205.5 2.0 fusion.191
  212.5 11.9 %scatter_custom_fusion.3 = bf16[896,128]{1,0:T(8,128)(2,1)S(1)} fusion(s32[2048]{0:T(1024)} %get-tuple-element.120, bf16[2048,128]{1,0:T(8,128)(2,1)} %copy.99, bf16[]{:T(256)} %constant.59.clone.1), kind=kCustom, calls=%fused_computation.261 | custom fusion | flops 262144 | bytes 229888 | tf_op jit(solution)/shard_map/transpose(jvp())/scatter-add | solution.py:37
  226.9 3.4 collective-permute-start.12
  231.6 4.6 collective-permute-start.14
  237.4 11.9 %scatter_fusion = bf16[512,128]{1,0:T(8,128)(2,1)S(1)} fusion(bf16[512,128]{1,0:T(8,128)(2,1)S(1)} %slice_add_fusion.2, s32[2048]{0:T(1024)} %get-tuple-element.117, bf16[2048,128]{1,0:T(8,128)(2,1)S(1)} %copy.100), kind=kCustom, calls=%fused_computation.16 | custom fusion | flops 262144 | bytes 1581056 | tf_op jit(solution)/shard_map/transpose(jvp())/scatter-add | solution.py:37
  254.9 1.6 constant_dynamic-update-slice_fusion.25
  264.3 3.6 stack.26
  267.9 3.2 scatter_custom_fusion.5
  272.7 1.9 fusion.43
  274.6 1.6 fusion.194
  279.9 7.6 %gather_fusion.10 = f32[2048,128]{1,0:T(8,128)} fusion(f32[512,128]{1,0:T(8,128)S(1)} %fusion.21, s32[2048]{0:T(1024)S(1)} %copy-done.70), kind=kCustom, calls=%fused_computation.10 | custom fusion | bytes 2105344 | tf_op jit(solution)/shard_map/transpose(jvp())/gather | solution.py:49
  287.6 1.6 copy.103
  289.2 2.0 multiply_reduce_fusion.1
  291.3 1.6 fusion.161
  294.7 2.0 fusion.193
  301.4 11.9 %scatter_custom_fusion.6 = bf16[896,128]{1,0:T(8,128)(2,1)S(1)} fusion(s32[2048]{0:T(1024)} %get-tuple-element.120, bf16[2048,128]{1,0:T(8,128)(2,1)} %copy.105, bf16[]{:T(256)} %constant.59.clone.1), kind=kCustom, calls=%fused_computation.259 | custom fusion | flops 262144 | bytes 229888 | tf_op jit(solution)/shard_map/transpose(jvp())/scatter-add | solution.py:37
  315.9 11.8 %scatter_fusion.1 = bf16[512,128]{1,0:T(8,128)(2,1)S(1)} fusion(bf16[512,128]{1,0:T(8,128)(2,1)S(1)} %slice_add_fusion.1, s32[2048]{0:T(1024)} %get-tuple-element.117, bf16[2048,128]{1,0:T(8,128)(2,1)S(1)} %copy.106), kind=kCustom, calls=%fused_computation.19 | custom fusion | flops 262144 | bytes 1581056 | tf_op jit(solution)/shard_map/transpose(jvp())/scatter-add | solution.py:37
  328.7 2.7 collective-permute-start.16
  332.8 4.3 collective-permute-start.18
  344.0 1.6 constant_dynamic-update-slice_fusion.24
  352.6 3.6 stack.25
  356.2 2.9 scatter_custom_fusion.8
  362.8 1.6 fusion.196
  368.5 8.4 %gather_fusion.11 = f32[2048,128]{1,0:T(8,128)} fusion(f32[512,128]{1,0:T(8,128)S(1)} %fusion.23, s32[2048]{0:T(1024)} %get-tuple-element.119), kind=kCustom, calls=%fused_computation.11 | custom fusion | bytes 2105344 | tf_op jit(solution)/shard_map/transpose(jvp())/gather | solution.py:49
  376.9 2.6 copy.109
  379.5 2.0 multiply_reduce_fusion.2
  385.4 1.6 convolution_convert_fusion
  387.2 2.5 stack.24
  389.7 2.4 pad_maximum_fusion
  392.2 11.9 %scatter_custom_fusion.9 = bf16[896,128]{1,0:T(8,128)(2,1)S(1)} fusion(s32[2048]{0:T(1024)} %get-tuple-element.120, bf16[2048,384]{1,0:T(8,128)(2,1)S(1)} %convolution_convert_fusion, bf16[]{:T(256)} %constant.59.clone.1), kind=kCustom, calls=%fused_computation.171 | custom fusion | flops 262144 | bytes 754176 | tf_op jit(solution)/shard_map/transpose(jvp())/scatter-add | solution.py:37
  404.1 12.0 %scatter_custom_fusion.10 = bf16[512,128]{1,0:T(8,128)(2,1)S(1)} fusion(bf16[512,128]{1,0:T(8,128)(2,1)S(1)} %slice_add_fusion, s32[2048]{0:T(1024)} %get-tuple-element.117, bf16[2048,384]{1,0:T(8,128)(2,1)S(1)} %convolution_convert_fusion), kind=kCustom, calls=%fused_computation.169 | custom fusion | flops 262144 | bytes 655360 | tf_op jit(solution)/shard_map/transpose(jvp())/scatter-add | solution.py:37
  416.1 4.0 collective-permute-start.20
  421.4 4.3 collective-permute-start.22
  427.3 4.2 collective-permute-done.23
  431.5 2.9 scatter_custom_fusion.11
  434.4 96.1 %all-reduce.2.cloned.1.call-done = f32[3,131840]{1,0:T(4,128)} async-done(((f32[3,131840]{1,0:T(4,128)}), f32[3,131840]{1,0:T(4,128)}) %all-reduce.2.cloned.1.call-update) | async-done | bytes 1582096 | tf_op jit(solution)/shard_map/psum | solution.py:164
  530.5 1.7 fusion.167
  533.1 2.3 fusion.165
  536.1 2.4 fusion.168
  (491 shorter events, 138.4 us)
Async XLA Ops:
  7.2 22.1 %copy-start = (bf16[512,128]{1,0:T(8,128)(2,1)S(1)}, bf16[512,128]{1,0:T(8,128)(2,1)}, u32[]{:S(2)}) copy-start(bf16[512,128]{1,0:T(8,128)(2,1)} %param.19) | copy-start | bytes 393220
  7.2 17.3 %copy-start.105 = (f32[3,128]{1,0:T(4,128)S(1)}, f32[3,128]{1,0:T(4,128)}, u32[]{:S(2)}) copy-start(f32[3,128]{1,0:T(4,128)} %param.27) | copy-start | bytes 4612
  7.2 17.9 %copy-start.106 = (f32[3,128]{1,0:T(4,128)S(1)}, f32[3,128]{1,0:T(4,128)}, u32[]{:S(2)}) copy-start(f32[3,128]{1,0:T(4,128)} %param.29) | copy-start | bytes 4612
  7.2 18.4 %copy-start.107 = (f32[3,128]{1,0:T(4,128)S(1)}, f32[3,128]{1,0:T(4,128)}, u32[]{:S(2)}) copy-start(f32[3,128]{1,0:T(4,128)} %param.30) | copy-start | bytes 4612
  7.2 19.0 %copy-start.108 = (f32[3,128]{1,0:T(4,128)S(1)}, f32[3,128]{1,0:T(4,128)}, u32[]{:S(2)}) copy-start(f32[3,128]{1,0:T(4,128)} %param.32) | copy-start | bytes 4612
  7.2 19.5 %copy-start.109 = (f32[3,128]{1,0:T(4,128)S(1)}, f32[3,128]{1,0:T(4,128)}, u32[]{:S(2)}) copy-start(f32[3,128]{1,0:T(4,128)} %param.34) | copy-start | bytes 4612
  7.2 20.1 %copy-start.110 = (f32[3,128]{1,0:T(4,128)S(1)}, f32[3,128]{1,0:T(4,128)}, u32[]{:S(2)}) copy-start(f32[3,128]{1,0:T(4,128)} %param.35) | copy-start | bytes 4612
  7.3 20.7 %copy-start.95 = (s32[2048]{0:T(1024)S(1)}, s32[2048]{0:T(1024)}, u32[]{:S(2)}) copy-start(s32[2048]{0:T(1024)} %param.21) | copy-start | bytes 24580
  7.3 21.3 %copy-start.84 = (s32[2048]{0:T(1024)S(1)}, s32[2048]{0:T(1024)}, u32[]{:S(2)}) copy-start(s32[2048]{0:T(1024)} %param.22) | copy-start | bytes 24580
  7.3 21.9 %copy-start.18 = (bf16[2048,128]{1,0:T(8,128)(2,1)S(1)}, bf16[2048,128]{1,0:T(8,128)(2,1)}, u32[]{:S(2)}) copy-start(bf16[2048,128]{1,0:T(8,128)(2,1)} %param.20) | copy-start | bytes 1572868
  7.3 523.3 %all-reduce.2.cloned.1.call-start = ((), (), s32[]{:S(2)}) async-start(), calls=%async_computation | async-start | bytes 4218880 | tf_op jit(solution)/shard_map/psum | solution.py:164
  8.1 22.2 %copy-start.96 = (s32[384]{0:T(512)}, s32[384]{0:T(512)S(1)}, u32[]{:S(2)}) copy-start(s32[384]{0:T(512)S(1)} %compare_select_fusion.2) | copy-start | bytes 4612
  9.1 19.4 %copy-start.23 = (bf16[512,128]{0,1:T(8,128)(2,1)}, bf16[512,128]{0,1:T(8,128)(2,1)S(1)}, u32[]{:S(2)}) copy-start(bf16[512,128]{0,1:T(8,128)(2,1)S(1)} %copy.72) | copy-start | bytes 393220
  9.3 21.0 %copy-start.104 = (s32[512]{0:T(512)S(1)}, s32[512]{0:T(512)}, u32[]{:S(2)}) copy-start(s32[512]{0:T(512)} %param.24) | copy-start | bytes 6148
  9.3 21.0 %copy-start.97 = (s32[2048]{0:T(1024)S(1)}, s32[2048]{0:T(1024)}, u32[]{:S(2)}) copy-start(s32[2048]{0:T(1024)} %param.23) | copy-start | bytes 24580
  9.3 21.0 %copy-start.56 = (f32[3,128,128]{2,1,0:T(8,128)S(1)}, f32[3,128,128]{2,1,0:T(8,128)}, u32[]{:S(2)}) copy-start(f32[3,128,128]{2,1,0:T(8,128)} %param.28) | copy-start | bytes 589828
  10.8 20.2 %copy-start.57 = (f32[3,128,128]{2,1,0:T(8,128)S(1)}, f32[3,128,128]{2,1,0:T(8,128)}, u32[]{:S(2)}) copy-start(f32[3,128,128]{2,1,0:T(8,128)} %param.33) | copy-start | bytes 589828
  11.4 29.1 %collective-permute-start.1 = (bf16[64,128]{1,0:T(8,128)(2,1)}, bf16[64,128]{1,0:T(8,128)(2,1)}, u32[]{:S(2)}, u32[]{:S(2)}) collective-permute-start(bf16[64,128]{1,0:T(8,128)(2,1)} %get-tuple-element.115), channel_id=1, source_target_pairs={{1,0},{2,1},{3,2},{5,4},{6,5},{7,6},{9,8},{10,9},{11,10},{13,12},{... | collective-permute-start | bytes 49160 | tf_op jit(solution)/shard_map/ppermute | solution.py:10
  12.7 19.0 %copy-start.58 = (f32[3,128,128]{2,1,0:T(8,128)S(1)}, f32[3,128,128]{2,1,0:T(8,128)}, u32[]{:S(2)}) copy-start(f32[3,128,128]{2,1,0:T(8,128)} %param.36) | copy-start | bytes 589828
  12.7 27.1 %collective-permute-start = (bf16[64,128]{1,0:T(8,128)(2,1)}, bf16[64,128]{1,0:T(8,128)(2,1)}, u32[]{:S(2)}, u32[]{:S(2)}) collective-permute-start(bf16[64,128]{1,0:T(8,128)(2,1)} %get-tuple-element.116), channel_id=1, source_target_pairs={{0,1},{1,2},{2,3},{4,5},{5,6},{6,7},{8,9},{9,10},{10,11},{12,13},{... | collective-permute-start | bytes 49160 | tf_op jit(solution)/shard_map/ppermute | solution.py:10
  17.1 24.9 %collective-permute-start.3 = (bf16[128,128]{1,0:T(8,128)(2,1)}, bf16[128,128]{1,0:T(8,128)(2,1)S(1)}, u32[]{:S(2)}, u32[]{:S(2)}) collective-permute-start(bf16[128,128]{1,0:T(8,128)(2,1)} %get-tuple-element.113), channel_id=1, source_target_pairs={{4,0},{8,4},{12,8},{16,12},{20,16},{24,20},{28,24},{5,1},{9,5},{13... | collective-permute-start | bytes 98312 | tf_op jit(solution)/shard_map/ppermute | solution.py:10
  18.4 22.8 %collective-permute-start.2 = (bf16[128,128]{1,0:T(8,128)(2,1)}, bf16[128,128]{1,0:T(8,128)(2,1)}, u32[]{:S(2)}, u32[]{:S(2)}) collective-permute-start(bf16[128,128]{1,0:T(8,128)(2,1)} %get-tuple-element.114), channel_id=1, source_target_pairs={{0,4},{4,8},{8,12},{12,16},{16,20},{20,24},{24,28},{1,5},{5,9},{9,... | collective-permute-start | bytes 98312 | tf_op jit(solution)/shard_map/ppermute | solution.py:10
  32.3 33.3 %copy-start.41 = (bf16[3,256,128]{2,1,0:T(8,128)(2,1)}, bf16[3,256,128]{2,1,0:T(8,128)(2,1)S(1)}, u32[]{:S(2)}) copy-start(bf16[3,256,128]{2,1,0:T(8,128)(2,1)S(1)} %convert.42) | copy-start | bytes 589828
  33.5 15.0 %copy-start.19 = (bf16[3,384,128]{2,1,0:T(8,128)(2,1)}, bf16[3,384,128]{2,1,0:T(8,128)(2,1)S(1)}, u32[]{:S(2)}) copy-start(bf16[3,384,128]{2,1,0:T(8,128)(2,1)S(1)} %convert.40) | copy-start | bytes 884740
  67.0 14.9 %copy-start.78 = (f32[512]{0:T(512)}, f32[512]{0:T(512)S(1)}, u32[]{:S(2)}) copy-start(f32[512]{0:T(512)S(1)} %broadcast_multiply_fusion.5) | copy-start | bytes 6148
  67.0 14.9 %copy-start.66 = (s32[2048]{0:T(1024)S(1)}, s32[2048]{0:T(1024)}, u32[]{:S(2)}) copy-start(s32[2048]{0:T(1024)} %copy-done.65) | copy-start | bytes 24580
  67.1 21.1 %copy-start.88 = (f32[512]{0:T(512)}, f32[512]{0:T(512)S(1)}, u32[]{:S(2)}) copy-start(f32[512]{0:T(512)S(1)} %multiply_reduce_fusion.17) | copy-start | bytes 6148
  67.1 21.1 %copy-start.81 = (f32[512]{0:T(512)}, f32[512]{0:T(512)S(1)}, u32[]{:S(2)}) copy-start(f32[512]{0:T(512)S(1)} %fusion.145) | copy-start | bytes 6148
  68.2 21.7 %copy-start.25 = (bf16[512,128]{0,1:T(8,128)(2,1)}, bf16[512,128]{0,1:T(8,128)(2,1)S(1)}, u32[]{:S(2)}) copy-start(bf16[512,128]{0,1:T(8,128)(2,1)S(1)} %get-tuple-element.144) | copy-start | bytes 393220
  69.9 19.4 %collective-permute-start.7 = (bf16[128,128]{0,1:T(8,128)(2,1)S(1)}, bf16[128,128]{0,1:T(8,128)(2,1)}, u32[]{:S(2)}, u32[]{:S(2)}) collective-permute-start(bf16[128,128]{0,1:T(8,128)(2,1)S(1)} %get-tuple-element.109), channel_id=1, source_target_pairs={{4,0},{8,4},{12,8},{16,12},{20,16},{24,20},{28,24},{5,1},{9,5},{13... | collective-permute-start | bytes 98312 | tf_op jit(solution)/shard_map/ppermute | solution.py:10
  71.2 18.7 %collective-permute-start.6 = (bf16[128,128]{0,1:T(8,128)(2,1)S(1)}, bf16[128,128]{0,1:T(8,128)(2,1)}, u32[]{:S(2)}, u32[]{:S(2)}) collective-permute-start(bf16[128,128]{0,1:T(8,128)(2,1)S(1)} %get-tuple-element.110), channel_id=1, source_target_pairs={{0,4},{4,8},{8,12},{12,16},{16,20},{20,24},{24,28},{1,5},{5,9},{9,... | collective-permute-start | bytes 98312 | tf_op jit(solution)/shard_map/ppermute | solution.py:10
  77.3 12.0 %collective-permute-start.5 = (bf16[64,128]{0,1:T(8,128)(2,1)}, bf16[64,128]{0,1:T(8,128)(2,1)S(1)}, u32[]{:S(2)}, u32[]{:S(2)}) collective-permute-start(bf16[64,128]{0,1:T(8,128)(2,1)} %get-tuple-element.111), channel_id=1, source_target_pairs={{1,0},{2,1},{3,2},{5,4},{6,5},{7,6},{9,8},{10,9},{11,10},{13,12},{... | collective-permute-start | bytes 49160 | tf_op jit(solution)/shard_map/ppermute | solution.py:10
  78.6 10.7 %collective-permute-start.4 = (bf16[64,128]{0,1:T(8,128)(2,1)S(1)}, bf16[64,128]{0,1:T(8,128)(2,1)S(1)}, u32[]{:S(2)}, u32[]{:S(2)}) collective-permute-start(bf16[64,128]{0,1:T(8,128)(2,1)S(1)} %get-tuple-element.112), channel_id=1, source_target_pairs={{0,1},{1,2},{2,3},{4,5},{5,6},{6,7},{8,9},{9,10},{10,11},{12,13},{... | collective-permute-start | bytes 49160 | tf_op jit(solution)/shard_map/ppermute | solution.py:10
  104.0 14.6 %copy-start.26 = (bf16[512,128]{0,1:T(8,128)(2,1)S(1)}, bf16[512,128]{0,1:T(8,128)(2,1)}, u32[]{:S(2)}) copy-start(bf16[512,128]{0,1:T(8,128)(2,1)} %copy-done.25) | copy-start | bytes 393220
  104.0 14.6 %copy-start.114 = (f32[128]{0:T(128)S(1)}, f32[128]{0:T(128)}, u32[]{:S(2)}) copy-start(f32[128]{0:T(128)} %get-tuple-element.127) | copy-start | bytes 1540
  104.0 15.8 %copy-start.115 = (f32[128]{0:T(128)S(1)}, f32[128]{0:T(128)}, u32[]{:S(2)}) copy-start(f32[128]{0:T(128)} %get-tuple-element.130) | copy-start | bytes 1540
  120.9 16.6 %copy-start.38 = (f32[512,128]{1,0:T(8,128)S(1)}, f32[512,128]{1,0:T(8,128)}, u32[]{:S(2)}) copy-start(f32[512,128]{1,0:T(8,128)} %param.37) | copy-start | bytes 786436
  121.0 16.6 %copy-start.89 = (f32[512]{0:T(512)}, f32[512]{0:T(512)S(1)}, u32[]{:S(2)}) copy-start(f32[512]{0:T(512)S(1)} %multiply_reduce_fusion.16) | copy-start | bytes 6148
  122.1 22.8 %copy-start.13 = (f32[512,128]{0,1:T(8,128)}, f32[512,128]{0,1:T(8,128)S(1)}, u32[]{:S(2)}) copy-start(f32[512,128]{0,1:T(8,128)S(1)} %get-tuple-element.151) | copy-start | bytes 786436
  122.1 23.8 %copy-start.30 = (bf16[512,128]{0,1:T(8,128)(2,1)}, bf16[512,128]{0,1:T(8,128)(2,1)S(1)}, u32[]{:S(2)}) copy-start(bf16[512,128]{0,1:T(8,128)(2,1)S(1)} %get-tuple-element.150) | copy-start | bytes 393220
  125.2 20.8 %collective-permute-start.9 = (bf16[64,128]{0,1:T(8,128)(2,1)}, bf16[64,128]{0,1:T(8,128)(2,1)}, u32[]{:S(2)}, u32[]{:S(2)}) collective-permute-start(bf16[64,128]{0,1:T(8,128)(2,1)} %get-tuple-element.107), channel_id=1, source_target_pairs={{1,0},{2,1},{3,2},{5,4},{6,5},{7,6},{9,8},{10,9},{11,10},{13,12},{... | collective-permute-start | bytes 49160 | tf_op jit(solution)/shard_map/ppermute | solution.py:10
  126.5 19.5 %collective-permute-start.8 = (bf16[64,128]{0,1:T(8,128)(2,1)}, bf16[64,128]{0,1:T(8,128)(2,1)}, u32[]{:S(2)}, u32[]{:S(2)}) collective-permute-start(bf16[64,128]{0,1:T(8,128)(2,1)} %get-tuple-element.108), channel_id=1, source_target_pairs={{0,1},{1,2},{2,3},{4,5},{5,6},{6,7},{8,9},{9,10},{10,11},{12,13},{... | collective-permute-start | bytes 49160 | tf_op jit(solution)/shard_map/ppermute | solution.py:10
  130.9 15.1 %collective-permute-start.11 = (bf16[128,128]{0,1:T(8,128)(2,1)}, bf16[128,128]{0,1:T(8,128)(2,1)}, u32[]{:S(2)}, u32[]{:S(2)}) collective-permute-start(bf16[128,128]{0,1:T(8,128)(2,1)} %get-tuple-element.105), channel_id=1, source_target_pairs={{4,0},{8,4},{12,8},{16,12},{20,16},{24,20},{28,24},{5,1},{9,5},{13... | collective-permute-start | bytes 98312 | tf_op jit(solution)/shard_map/ppermute | solution.py:10
  132.2 13.8 %collective-permute-start.10 = (bf16[128,128]{0,1:T(8,128)(2,1)}, bf16[128,128]{0,1:T(8,128)(2,1)}, u32[]{:S(2)}, u32[]{:S(2)}) collective-permute-start(bf16[128,128]{0,1:T(8,128)(2,1)} %get-tuple-element.106), channel_id=1, source_target_pairs={{0,4},{4,8},{8,12},{12,16},{16,20},{20,24},{24,28},{1,5},{5,9},{9,... | collective-permute-start | bytes 98312 | tf_op jit(solution)/shard_map/ppermute | solution.py:10
  137.6 46.4 %copy-start.5 = (f32[512,128]{0,1:T(8,128)}, f32[512,128]{0,1:T(8,128)S(1)}, u32[]{:S(2)}) copy-start(f32[512,128]{0,1:T(8,128)S(1)} %copy.95) | copy-start | bytes 786436
  226.9 41.0 %collective-permute-start.12 = (bf16[64,128]{1,0:T(8,128)(2,1)}, bf16[64,128]{1,0:T(8,128)(2,1)}, u32[]{:S(2)}, u32[]{:S(2)}) collective-permute-start(bf16[64,128]{1,0:T(8,128)(2,1)} %get-tuple-element.101), channel_id=1, source_target_pairs={{0,1},{1,2},{2,3},{4,5},{5,6},{6,7},{8,9},{9,10},{10,11},{12,13},{... | collective-permute-start | bytes 49160 | tf_op jit(solution)/shard_map/ppermute | solution.py:10
  230.3 37.6 %collective-permute-start.13 = (bf16[64,128]{1,0:T(8,128)(2,1)}, bf16[64,128]{1,0:T(8,128)(2,1)}, u32[]{:S(2)}, u32[]{:S(2)}) collective-permute-start(bf16[64,128]{1,0:T(8,128)(2,1)} %get-tuple-element.102), channel_id=1, source_target_pairs={{1,0},{2,1},{3,2},{5,4},{6,5},{7,6},{9,8},{10,9},{11,10},{13,12},{... | collective-permute-start | bytes 49160 | tf_op jit(solution)/shard_map/ppermute | solution.py:10
  231.6 36.3 %collective-permute-start.14 = (bf16[128,128]{1,0:T(8,128)(2,1)}, bf16[128,128]{1,0:T(8,128)(2,1)}, u32[]{:S(2)}, u32[]{:S(2)}) collective-permute-start(bf16[128,128]{1,0:T(8,128)(2,1)} %get-tuple-element.103), channel_id=1, source_target_pairs={{0,4},{4,8},{8,12},{12,16},{16,20},{20,24},{24,28},{1,5},{5,9},{9,... | collective-permute-start | bytes 98312 | tf_op jit(solution)/shard_map/ppermute | solution.py:10
  236.1 31.8 %collective-permute-start.15 = (bf16[128,128]{1,0:T(8,128)(2,1)}, bf16[128,128]{1,0:T(8,128)(2,1)}, u32[]{:S(2)}, u32[]{:S(2)}) collective-permute-start(bf16[128,128]{1,0:T(8,128)(2,1)} %get-tuple-element.104), channel_id=1, source_target_pairs={{4,0},{8,4},{12,8},{16,12},{20,16},{24,20},{28,24},{5,1},{9,5},{13... | collective-permute-start | bytes 98312 | tf_op jit(solution)/shard_map/ppermute | solution.py:10
  237.4 26.1 %copy-start.32 = (f32[512,128]{0,1:T(8,128)S(1)}, f32[512,128]{0,1:T(8,128)}, u32[]{:S(2)}) copy-start(f32[512,128]{0,1:T(8,128)} %fusion.3) | copy-start | bytes 786436
  249.4 21.9 %copy-start.12 = (f32[512,128]{0,1:T(8,128)S(1)}, f32[512,128]{0,1:T(8,128)}, u32[]{:S(2)}) copy-start(f32[512,128]{0,1:T(8,128)} %copy-done.11) | copy-start | bytes 786436
  249.4 21.9 %copy-start.80 = (f32[512]{0:T(512)S(1)}, f32[512]{0:T(512)}, u32[]{:S(2)}) copy-start(f32[512]{0:T(512)} %copy-done.79) | copy-start | bytes 6148
  249.4 21.9 %copy-start.83 = (f32[512]{0:T(512)S(1)}, f32[512]{0:T(512)}, u32[]{:S(2)}) copy-start(f32[512]{0:T(512)} %copy-done.82) | copy-start | bytes 6148
  249.4 21.9 %copy-start.99 = (f32[128]{0:T(128)S(1)}, f32[128]{0:T(128)}, u32[]{:S(2)}) copy-start(f32[128]{0:T(128)} %get-tuple-element.124) | copy-start | bytes 1540
  327.7 31.5 %copy-start.10 = (f32[512,128]{0,1:T(8,128)S(1)}, f32[512,128]{0,1:T(8,128)}, u32[]{:S(2)}) copy-start(f32[512,128]{0,1:T(8,128)} %copy-done.9) | copy-start | bytes 786436
  328.7 27.4 %collective-permute-start.16 = (bf16[64,128]{1,0:T(8,128)(2,1)}, bf16[64,128]{1,0:T(8,128)(2,1)S(1)}, u32[]{:S(2)}, u32[]{:S(2)}) collective-permute-start(bf16[64,128]{1,0:T(8,128)(2,1)} %get-tuple-element.97), channel_id=1, source_target_pairs={{0,1},{1,2},{2,3},{4,5},{5,6},{6,7},{8,9},{9,10},{10,11},{12,13},{... | collective-permute-start | bytes 49160 | tf_op jit(solution)/shard_map/ppermute | solution.py:10
  331.5 24.7 %collective-permute-start.17 = (bf16[64,128]{1,0:T(8,128)(2,1)}, bf16[64,128]{1,0:T(8,128)(2,1)S(1)}, u32[]{:S(2)}, u32[]{:S(2)}) collective-permute-start(bf16[64,128]{1,0:T(8,128)(2,1)} %get-tuple-element.98), channel_id=1, source_target_pairs={{1,0},{2,1},{3,2},{5,4},{6,5},{7,6},{9,8},{10,9},{11,10},{13,12},{... | collective-permute-start | bytes 49160 | tf_op jit(solution)/shard_map/ppermute | solution.py:10
  332.8 23.4 %collective-permute-start.18 = (bf16[128,128]{1,0:T(8,128)(2,1)}, bf16[128,128]{1,0:T(8,128)(2,1)S(1)}, u32[]{:S(2)}, u32[]{:S(2)}) collective-permute-start(bf16[128,128]{1,0:T(8,128)(2,1)} %get-tuple-element.99), channel_id=1, source_target_pairs={{0,4},{4,8},{8,12},{12,16},{16,20},{20,24},{24,28},{1,5},{5,9},{9,... | collective-permute-start | bytes 98312 | tf_op jit(solution)/shard_map/ppermute | solution.py:10
  337.1 19.1 %collective-permute-start.19 = (bf16[128,128]{1,0:T(8,128)(2,1)}, bf16[128,128]{1,0:T(8,128)(2,1)S(1)}, u32[]{:S(2)}, u32[]{:S(2)}) collective-permute-start(bf16[128,128]{1,0:T(8,128)(2,1)} %get-tuple-element.100), channel_id=1, source_target_pairs={{4,0},{8,4},{12,8},{16,12},{20,16},{24,20},{28,24},{5,1},{9,5},{13... | collective-permute-start | bytes 98312 | tf_op jit(solution)/shard_map/ppermute | solution.py:10
  416.1 11.0 %collective-permute-start.20 = (bf16[64,128]{1,0:T(8,128)(2,1)S(1)}, bf16[64,128]{1,0:T(8,128)(2,1)S(1)}, u32[]{:S(2)}, u32[]{:S(2)}) collective-permute-start(bf16[64,128]{1,0:T(8,128)(2,1)S(1)} %get-tuple-element.93), channel_id=1, source_target_pairs={{0,1},{1,2},{2,3},{4,5},{5,6},{6,7},{8,9},{9,10},{10,11},{12,13},{... | collective-permute-start | bytes 49160 | tf_op jit(solution)/shard_map/ppermute | solution.py:10
  420.1 6.9 %collective-permute-start.21 = (bf16[64,128]{1,0:T(8,128)(2,1)S(1)}, bf16[64,128]{1,0:T(8,128)(2,1)S(1)}, u32[]{:S(2)}, u32[]{:S(2)}) collective-permute-start(bf16[64,128]{1,0:T(8,128)(2,1)S(1)} %get-tuple-element.94), channel_id=1, source_target_pairs={{1,0},{2,1},{3,2},{5,4},{6,5},{7,6},{9,8},{10,9},{11,10},{13,12},{... | collective-permute-start | bytes 49160 | tf_op jit(solution)/shard_map/ppermute | solution.py:10
  421.4 5.9 %collective-permute-start.22 = (bf16[128,128]{1,0:T(8,128)(2,1)S(1)}, bf16[128,128]{1,0:T(8,128)(2,1)S(1)}, u32[]{:S(2)}, u32[]{:S(2)}) collective-permute-start(bf16[128,128]{1,0:T(8,128)(2,1)S(1)} %get-tuple-element.95), channel_id=1, source_target_pairs={{0,4},{4,8},{8,12},{12,16},{16,20},{20,24},{24,28},{1,5},{5,9},{9,... | collective-permute-start | bytes 98312 | tf_op jit(solution)/shard_map/ppermute | solution.py:10
  425.7 5.8 %collective-permute-start.23 = (bf16[128,128]{1,0:T(8,128)(2,1)S(1)}, bf16[128,128]{1,0:T(8,128)(2,1)S(1)}, u32[]{:S(2)}, u32[]{:S(2)}) collective-permute-start(bf16[128,128]{1,0:T(8,128)(2,1)S(1)} %get-tuple-element.96), channel_id=1, source_target_pairs={{4,0},{8,4},{12,8},{16,12},{20,16},{24,20},{28,24},{5,1},{9,5},{13... | collective-permute-start | bytes 98312 | tf_op jit(solution)/shard_map/ppermute | solution.py:10
  434.4 101.7 %copy-start.49 = (f32[512,128]{1,0:T(8,128)}, f32[512,128]{1,0:T(8,128)S(1)}, u32[]{:S(2)}) copy-start(f32[512,128]{1,0:T(8,128)S(1)} %scatter_custom_fusion.11) | copy-start | bytes 786436
  (92 other events, 311.6 us)
Sparse Core Ops, SparseCore 0:
  392.3 138.2 all-reduce.1
where the time goes:
time: 559 us; the launch traced here: 549 us
  local copies, waits for them, and re-layouts  161 us (29%)
  other arithmetic  151 us (27%)
  waiting for transfers between devices  101 us (18%)
  starting transfers between devices  67.2 us (12%)
  matrix products  52.3 us (9%)
  between operations  16.9 us (3%)
    psum x1, waiting for transfers between devices, on_device(): stacked = lax.psum(stacked, ('dom', 'sub'))  96.1 us
    ppermute x24, starting transfers between devices, passed_along(): lax.ppermute(value, axis, [(source, source + steps) for source in range(f...  67.2 us
    scatter-add x3, other arithmetic, layer_local(): jax.ops.segment_sum(message, receivers, num_segments=latent.shape[0])  36.7 us
    unnamed x299, local copies, waits for them, and re-layouts  36.6 us
    scatter-add x3, other arithmetic, layer_local(): extended[senders]  35.8 us
    scatter-add x3, other arithmetic, layer_local(): own[receivers]  35.6 us
    gather x6, local copies, waits for them, and re-layouts, layer_local(): jax.ops.segment_sum(message, receivers, num_segments=latent.shape[0])  31 us
    gather x5, local copies, waits for them, and re-layouts, layer_local(): extended[senders]  21.6 us
  transfers between devices with their start and end apart: 25, of which 3 were waited for; matrix products, arithmetic and copies ran while one was open for 20% of the time, Pallas kernels for 0%

commit v1 on v0

--- a/solution.py
+++ b/solution.py
@@ -161,7 +161,7 @@
         flat = flatten_all(weight_grads)
         per_layer[layer] = flat
     stacked = jnp.stack(per_layer, axis=0)
-    stacked = lax.psum(stacked, ("dom", "sub"))
+    stacked = lax.psum(lax.psum(stacked, "sub"), "dom")
     by_layer = [unflatten_all(stacked[layer], layer_shapes) for layer in range(layers)]
     results = [
         jnp.stack([by_layer[layer][which] for layer in range(layers)], axis=0)

time: 559 us -> 581 us (1.039)
  waiting for transfers between devices: 101 us -> 125 us
    psum x1 -> x2, waiting for transfers between devices: 96.1 us -> 120 us  [on_device(): stacked = lax.psum(lax.psum(stacked, 'sub'), 'dom')]
    unnamed x299 -> x317, local copies, waits for them, and re-layouts: 36.6 us -> 36 us
  transfers between devices with their start and end apart: 25 -> 26, of which waited for: 3 -> 4; matrix products, arithmetic and copies ran while one was open for 20% -> 20% of each run, Pallas kernels for 0% -> 0%
where the time goes in v1:
time: 581 us; the launch traced here: 571 us
  local copies, waits for them, and re-layouts  162 us (28%)
  other arithmetic  151 us (26%)
  waiting for transfers between devices  125 us (22%)
  starting transfers between devices  63.6 us (11%)
  matrix products  52.2 us (9%)
  between operations  17.1 us (3%)
    psum x2, waiting for transfers between devices, on_device(): stacked = lax.psum(lax.psum(stacked, 'sub'), 'dom')  120 us
    ppermute x24, starting transfers between devices, passed_along(): lax.ppermute(value, axis, [(source, source + steps) for source in range(f...  63.3 us
    scatter-add x3, other arithmetic, layer_local(): jax.ops.segment_sum(message, receivers, num_segments=latent.shape[0])  36.7 us
    unnamed x317, local copies, waits for them, and re-layouts  36 us
    scatter-add x3, other arithmetic, layer_local(): extended[senders]  35.6 us
    scatter-add x3, other arithmetic, layer_local(): own[receivers]  35.1 us
    gather x6, local copies, waits for them, and re-layouts, layer_local(): jax.ops.segment_sum(message, receivers, num_segments=latent.shape[0])  30.9 us
    gather x5, local copies, waits for them, and re-layouts, layer_local(): own[receivers]  22.7 us
  transfers between devices with their start and end apart: 26, of which 4 were waited for; matrix products, arithmetic and copies ran while one was open for 20% of the time, Pallas kernels for 0%

profile of v1, /device:TPU:0, one launch (start us, length us, event | category | flops | bytes accessed | tf_op | source)
XLA Modules:
  0.0 570.6 jit_solution(12645345929435236009)
XLA Ops:
  12.7 3.6 collective-permute-start
  18.2 6.1 %collective-permute-start.2 = (bf16[128,128]{1,0:T(8,128)(2,1)}, bf16[128,128]{1,0:T(8,128)(2,1)}, u32[]{:S(2)}, u32[]{:S(2)}) collective-permute-start(bf16[128,128]{1,0:T(8,128)(2,1)} %get-tuple-element.114), channel_id=1, source_target_pairs={{0,4},{4,8},{8,12},{12,16},{16,20},{20,24},{24,28},{1,5},{5,9},{9,... | collective-permute-start | bytes 98312 | tf_op jit(solution)/shard_map/ppermute | solution.py:10
  31.4 1.6 convert.44
  34.2 7.3 %gather_fusion.2 = bf16[2048,128]{1,0:T(8,128)(2,1)S(1)} fusion(bf16[512,128]{1,0:T(8,128)(2,1)S(1)} %copy-done, s32[2048]{0:T(1024)} %get-tuple-element.118), kind=kCustom, calls=%fused_computation.2 | custom fusion | bytes 1056768 | tf_op jit(solution)/shard_map/jvp()/gather | solution.py:37
  44.6 6.2 %gather_fusion.1 = bf16[2048,128]{1,0:T(8,128)(2,1)S(1)} fusion(bf16[896,128]{1,0:T(8,128)(2,1)S(1)} %constant_dynamic-update-slice_fusion, s32[2048]{0:T(1024)S(1)} %copy-done.61), kind=kCustom, calls=%fused_computation.1 | custom fusion | bytes 1056768 | tf_op jit(solution)/shard_map/jvp()/gather | solution.py:37
  56.2 11.9 %scatter_custom_fusion = f32[512,128]{1,0:T(8,128)S(1)} fusion(s32[2048]{0:T(1024)} %param.22, f32[2048,128]{1,0:T(8,128)} %copy.74, f32[]{:T(128)} %constant.51.clone.1), kind=kCustom, calls=%fused_computation.256 | custom fusion | flops 262144 | bytes 262656 | tf_op jit(solution)/shard_map/jvp()/scatter-add | solution.py:49
  73.7 5.5 collective-permute-start.6
  81.0 3.2 collective-permute-start.4
  84.4 6.2 %gather_fusion.5 = bf16[2048,128]{1,0:T(8,128)(2,1)S(1)} fusion(bf16[512,128]{1,0:T(8,128)(2,1)S(1)} %copy.80, s32[2048]{0:T(1024)S(1)} %copy-done.67), kind=kCustom, calls=%fused_computation.5 | custom fusion | bytes 1056768 | tf_op jit(solution)/shard_map/jvp()/gather | solution.py:37
  93.5 6.2 %gather_fusion.4 = bf16[2048,128]{1,0:T(8,128)(2,1)S(1)} fusion(bf16[896,128]{1,0:T(8,128)(2,1)S(1)} %copy.79, s32[2048]{0:T(1024)S(1)} %copy-done.62), kind=kCustom, calls=%fused_computation.4 | custom fusion | bytes 1056768 | tf_op jit(solution)/shard_map/jvp()/gather | solution.py:37
  100.7 2.0 convolution_add_fusion.3
  106.5 2.6 copy.83
  109.1 11.9 %scatter_custom_fusion.1 = f32[512,128]{1,0:T(8,128)S(1)} fusion(s32[2048]{0:T(1024)S(1)} %copy-done.92, f32[2048,128]{1,0:T(8,128)} %copy.83, f32[]{:T(128)} %constant.51.clone.1), kind=kCustom, calls=%fused_computation.254 | custom fusion | flops 262144 | bytes 262656 | tf_op jit(solution)/shard_map/jvp()/scatter-add | solution.py:49
  128.9 4.4 collective-permute-start.8
  134.7 5.3 collective-permute-start.10
  140.2 7.2 %gather_fusion.8 = bf16[2048,128]{1,0:T(8,128)(2,1)S(1)} fusion(bf16[512,128]{1,0:T(8,128)(2,1)S(1)} %copy.89, s32[2048]{0:T(1024)} %get-tuple-element.118), kind=kCustom, calls=%fused_computation.8 | custom fusion | bytes 1056768 | tf_op jit(solution)/shard_map/jvp()/gather | solution.py:37
  149.5 7.2 %gather_fusion.7 = bf16[2048,128]{1,0:T(8,128)(2,1)S(1)} fusion(bf16[896,128]{1,0:T(8,128)(2,1)S(1)} %copy.88, s32[2048]{0:T(1024)} %get-tuple-element.121), kind=kCustom, calls=%fused_computation.7 | custom fusion | bytes 1056768 | tf_op jit(solution)/shard_map/jvp()/gather | solution.py:37
  157.7 2.0 convolution_add_fusion.1
  163.6 2.5 copy.92
  166.1 12.9 %scatter_custom_fusion.2 = f32[512,128]{1,0:T(8,128)} fusion(s32[2048]{0:T(1024)} %param.22, f32[2048,128]{1,0:T(8,128)} %copy.92, f32[]{:T(128)} %constant.51.clone.1), kind=kCustom, calls=%fused_computation.252 | custom fusion | flops 262144 | bytes 262656 | tf_op jit(solution)/shard_map/jvp()/scatter-add | solution.py:49
  179.0 1.7 copy.93
  180.7 1.7 fusion.37
  187.3 1.6 fusion.192
  191.9 8.3 %gather_fusion.9 = f32[2048,128]{1,0:T(8,128)} fusion(f32[512,128]{1,0:T(8,128)S(1)} %fusion.19, s32[2048]{0:T(1024)} %get-tuple-element.119), kind=kCustom, calls=%fused_computation.9 | custom fusion | bytes 2105344 | tf_op jit(solution)/shard_map/transpose(jvp())/gather | solution.py:49
  200.2 2.6 copy.97
  202.9 2.3 multiply_reduce_fusion
  214.0 11.9 %scatter_custom_fusion.3 = bf16[896,128]{1,0:T(8,128)(2,1)S(1)} fusion(s32[2048]{0:T(1024)} %get-tuple-element.120, bf16[2048,128]{1,0:T(8,128)(2,1)} %copy.99, bf16[]{:T(256)} %constant.59.clone.1), kind=kCustom, calls=%fused_computation.261 | custom fusion | flops 262144 | bytes 229888 | tf_op jit(solution)/shard_map/transpose(jvp())/scatter-add | solution.py:37
  228.4 2.8 collective-permute-start.12
  232.4 4.6 collective-permute-start.14
  238.3 11.6 %scatter_fusion = bf16[512,128]{1,0:T(8,128)(2,1)S(1)} fusion(bf16[512,128]{1,0:T(8,128)(2,1)S(1)} %slice_add_fusion.2, s32[2048]{0:T(1024)S(1)} %copy-done.73, bf16[2048,128]{1,0:T(8,128)(2,1)S(1)} %copy.100), kind=kCustom, calls=%fused_computation.16 | custom fusion | flops 262144 | bytes 1581056 | tf_op jit(solution)/shard_map/transpose(jvp())/scatter-add | solution.py:37
  251.4 1.5 constant_dynamic-update-slice_fusion.34
  255.5 1.6 constant_dynamic-update-slice_fusion.25
  264.1 3.6 stack.26
  267.7 3.2 scatter_custom_fusion.5
  273.4 1.6 fusion.194
  278.7 7.6 %gather_fusion.10 = f32[2048,128]{1,0:T(8,128)} fusion(f32[512,128]{1,0:T(8,128)S(1)} %fusion.21, s32[2048]{0:T(1024)S(1)} %copy-done.72), kind=kCustom, calls=%fused_computation.10 | custom fusion | bytes 2105344 | tf_op jit(solution)/shard_map/transpose(jvp())/gather | solution.py:49
  286.3 1.6 copy.103
  287.9 2.0 multiply_reduce_fusion.1
  290.0 1.6 fusion.161
  293.3 2.0 fusion.193
  300.0 11.9 %scatter_custom_fusion.6 = bf16[896,128]{1,0:T(8,128)(2,1)S(1)} fusion(s32[2048]{0:T(1024)} %get-tuple-element.120, bf16[2048,128]{1,0:T(8,128)(2,1)} %copy.105, bf16[]{:T(256)} %constant.59.clone.1), kind=kCustom, calls=%fused_computation.259 | custom fusion | flops 262144 | bytes 229888 | tf_op jit(solution)/shard_map/transpose(jvp())/scatter-add | solution.py:37
  314.5 11.8 %scatter_fusion.1 = bf16[512,128]{1,0:T(8,128)(2,1)S(1)} fusion(bf16[512,128]{1,0:T(8,128)(2,1)S(1)} %slice_add_fusion.1, s32[2048]{0:T(1024)} %get-tuple-element.117, bf16[2048,128]{1,0:T(8,128)(2,1)S(1)} %copy.106), kind=kCustom, calls=%fused_computation.19 | custom fusion | flops 262144 | bytes 1581056 | tf_op jit(solution)/shard_map/transpose(jvp())/scatter-add | solution.py:37
  327.3 2.8 collective-permute-start.16
  331.5 4.3 collective-permute-start.18
  342.7 1.6 constant_dynamic-update-slice_fusion.24
  351.3 3.6 stack.25
  354.9 2.9 scatter_custom_fusion.8
  361.4 1.6 fusion.196
  367.8 8.3 %gather_fusion.11 = f32[2048,128]{1,0:T(8,128)} fusion(f32[512,128]{1,0:T(8,128)S(1)} %fusion.23, s32[2048]{0:T(1024)} %get-tuple-element.119), kind=kCustom, calls=%fused_computation.11 | custom fusion | bytes 2105344 | tf_op jit(solution)/shard_map/transpose(jvp())/gather | solution.py:49
  376.1 2.6 copy.109
  378.7 2.0 multiply_reduce_fusion.2
  385.0 2.5 stack.24
  387.5 2.4 pad_maximum_fusion
  390.3 56.3 %all-reduce.3.cloned.1.call-done = f32[3,131840]{1,0:T(4,128)} async-done(((f32[3,131840]{1,0:T(4,128)}), f32[3,131840]{1,0:T(4,128)}) %all-reduce.3.cloned.1.call-update) | async-done | bytes 1582096 | tf_op jit(solution)/shard_map/psum | solution.py:164
  450.0 11.7 %scatter_custom_fusion.9 = bf16[896,128]{1,0:T(8,128)(2,1)S(1)} fusion(s32[2048]{0:T(1024)} %get-tuple-element.120, bf16[2048,384]{1,0:T(8,128)(2,1)S(1)} %convolution_convert_fusion, bf16[]{:T(256)} %constant.59.clone.1), kind=kCustom, calls=%fused_computation.171 | custom fusion | flops 262144 | bytes 754176 | tf_op jit(solution)/shard_map/transpose(jvp())/scatter-add | solution.py:37
  461.8 11.7 %scatter_custom_fusion.10 = bf16[512,128]{1,0:T(8,128)(2,1)S(1)} fusion(bf16[512,128]{1,0:T(8,128)(2,1)S(1)} %slice_add_fusion, s32[2048]{0:T(1024)} %get-tuple-element.117, bf16[2048,384]{1,0:T(8,128)(2,1)S(1)} %convolution_convert_fusion), kind=kCustom, calls=%fused_computation.169 | custom fusion | flops 262144 | bytes 655360 | tf_op jit(solution)/shard_map/transpose(jvp())/scatter-add | solution.py:37
  473.5 1.6 collective-permute-start.20
  476.5 3.4 collective-permute-start.22
  481.4 4.3 collective-permute-done.23
  485.7 2.9 scatter_custom_fusion.11
  488.6 64.0 %all-reduce.5.cloned.1.call-done = f32[3,131840]{1,0:T(4,128)} async-done(((f32[3,131840]{1,0:T(4,128)}), f32[3,131840]{1,0:T(4,128)}) %all-reduce.5.cloned.1.call-update) | async-done | bytes 1582096 | tf_op jit(solution)/shard_map/psum | solution.py:164
  552.6 1.8 fusion.167
  555.1 2.3 fusion.165
  558.1 2.2 fusion.168
  (512 shorter events, 142.0 us)
Async XLA Ops:
  7.2 21.9 %copy-start = (bf16[512,128]{1,0:T(8,128)(2,1)S(1)}, bf16[512,128]{1,0:T(8,128)(2,1)}, u32[]{:S(2)}) copy-start(bf16[512,128]{1,0:T(8,128)(2,1)} %param.19) | copy-start | bytes 393220
  7.2 17.7 %copy-start.115 = (f32[3,128]{1,0:T(4,128)S(1)}, f32[3,128]{1,0:T(4,128)}, u32[]{:S(2)}) copy-start(f32[3,128]{1,0:T(4,128)} %param.29) | copy-start | bytes 4612
  7.2 18.2 %copy-start.116 = (f32[3,128]{1,0:T(4,128)S(1)}, f32[3,128]{1,0:T(4,128)}, u32[]{:S(2)}) copy-start(f32[3,128]{1,0:T(4,128)} %param.30) | copy-start | bytes 4612
  7.2 18.8 %copy-start.117 = (f32[3,128]{1,0:T(4,128)S(1)}, f32[3,128]{1,0:T(4,128)}, u32[]{:S(2)}) copy-start(f32[3,128]{1,0:T(4,128)} %param.32) | copy-start | bytes 4612
  7.2 19.4 %copy-start.118 = (f32[3,128]{1,0:T(4,128)S(1)}, f32[3,128]{1,0:T(4,128)}, u32[]{:S(2)}) copy-start(f32[3,128]{1,0:T(4,128)} %param.34) | copy-start | bytes 4612
  7.2 19.9 %copy-start.119 = (f32[3,128]{1,0:T(4,128)S(1)}, f32[3,128]{1,0:T(4,128)}, u32[]{:S(2)}) copy-start(f32[3,128]{1,0:T(4,128)} %param.35) | copy-start | bytes 4612
  7.3 20.5 %copy-start.103 = (s32[2048]{0:T(1024)S(1)}, s32[2048]{0:T(1024)}, u32[]{:S(2)}) copy-start(s32[2048]{0:T(1024)} %param.21) | copy-start | bytes 24580
  7.3 21.1 %copy-start.91 = (s32[2048]{0:T(1024)S(1)}, s32[2048]{0:T(1024)}, u32[]{:S(2)}) copy-start(s32[2048]{0:T(1024)} %param.22) | copy-start | bytes 24580
  7.3 21.7 %copy-start.20 = (bf16[2048,128]{1,0:T(8,128)(2,1)S(1)}, bf16[2048,128]{1,0:T(8,128)(2,1)}, u32[]{:S(2)}) copy-start(bf16[2048,128]{1,0:T(8,128)(2,1)} %param.20) | copy-start | bytes 1572868
  7.3 439.3 %all-reduce.3.cloned.1.call-start = ((), (), s32[]{:S(2)}) async-start(), calls=%async_computation | async-start | bytes 4218880 | tf_op jit(solution)/shard_map/psum | solution.py:164
  8.1 20.9 %copy-start.104 = (s32[384]{0:T(512)}, s32[384]{0:T(512)S(1)}, u32[]{:S(2)}) copy-start(s32[384]{0:T(512)S(1)} %compare_select_fusion.2) | copy-start | bytes 4612
  9.2 20.9 %copy-start.26 = (bf16[512,128]{0,1:T(8,128)(2,1)}, bf16[512,128]{0,1:T(8,128)(2,1)S(1)}, u32[]{:S(2)}) copy-start(bf16[512,128]{0,1:T(8,128)(2,1)S(1)} %copy.72) | copy-start | bytes 393220
  9.3 20.8 %copy-start.113 = (s32[512]{0:T(512)S(1)}, s32[512]{0:T(512)}, u32[]{:S(2)}) copy-start(s32[512]{0:T(512)} %param.24) | copy-start | bytes 6148
  9.3 20.8 %copy-start.105 = (s32[2048]{0:T(1024)S(1)}, s32[2048]{0:T(1024)}, u32[]{:S(2)}) copy-start(s32[2048]{0:T(1024)} %param.23) | copy-start | bytes 24580
  9.3 20.8 %copy-start.59 = (f32[3,128,128]{2,1,0:T(8,128)S(1)}, f32[3,128,128]{2,1,0:T(8,128)}, u32[]{:S(2)}) copy-start(f32[3,128,128]{2,1,0:T(8,128)} %param.28) | copy-start | bytes 589828
  10.8 20.0 %copy-start.60 = (f32[3,128,128]{2,1,0:T(8,128)S(1)}, f32[3,128,128]{2,1,0:T(8,128)}, u32[]{:S(2)}) copy-start(f32[3,128,128]{2,1,0:T(8,128)} %param.33) | copy-start | bytes 589828
  11.4 30.9 %collective-permute-start.1 = (bf16[64,128]{1,0:T(8,128)(2,1)}, bf16[64,128]{1,0:T(8,128)(2,1)}, u32[]{:S(2)}, u32[]{:S(2)}) collective-permute-start(bf16[64,128]{1,0:T(8,128)(2,1)} %get-tuple-element.115), channel_id=1, source_target_pairs={{1,0},{2,1},{3,2},{5,4},{6,5},{7,6},{9,8},{10,9},{11,10},{13,12},{... | collective-permute-start | bytes 49160 | tf_op jit(solution)/shard_map/ppermute | solution.py:10
  12.7 28.9 %collective-permute-start = (bf16[64,128]{1,0:T(8,128)(2,1)}, bf16[64,128]{1,0:T(8,128)(2,1)}, u32[]{:S(2)}, u32[]{:S(2)}) collective-permute-start(bf16[64,128]{1,0:T(8,128)(2,1)} %get-tuple-element.116), channel_id=1, source_target_pairs={{0,1},{1,2},{2,3},{4,5},{5,6},{6,7},{8,9},{9,10},{10,11},{12,13},{... | collective-permute-start | bytes 49160 | tf_op jit(solution)/shard_map/ppermute | solution.py:10
  16.9 26.8 %collective-permute-start.3 = (bf16[128,128]{1,0:T(8,128)(2,1)}, bf16[128,128]{1,0:T(8,128)(2,1)}, u32[]{:S(2)}, u32[]{:S(2)}) collective-permute-start(bf16[128,128]{1,0:T(8,128)(2,1)} %get-tuple-element.113), channel_id=1, source_target_pairs={{4,0},{8,4},{12,8},{16,12},{20,16},{24,20},{28,24},{5,1},{9,5},{13... | collective-permute-start | bytes 98312 | tf_op jit(solution)/shard_map/ppermute | solution.py:10
  18.2 24.8 %collective-permute-start.2 = (bf16[128,128]{1,0:T(8,128)(2,1)}, bf16[128,128]{1,0:T(8,128)(2,1)}, u32[]{:S(2)}, u32[]{:S(2)}) collective-permute-start(bf16[128,128]{1,0:T(8,128)(2,1)} %get-tuple-element.114), channel_id=1, source_target_pairs={{0,4},{4,8},{8,12},{12,16},{16,20},{20,24},{24,28},{1,5},{5,9},{9,... | collective-permute-start | bytes 98312 | tf_op jit(solution)/shard_map/ppermute | solution.py:10
  33.0 35.1 %copy-start.42 = (bf16[3,256,128]{2,1,0:T(8,128)(2,1)}, bf16[3,256,128]{2,1,0:T(8,128)(2,1)S(1)}, u32[]{:S(2)}) copy-start(bf16[3,256,128]{2,1,0:T(8,128)(2,1)S(1)} %convert.42) | copy-start | bytes 589828
  69.6 21.1 %copy-start.95 = (f32[512]{0:T(512)}, f32[512]{0:T(512)S(1)}, u32[]{:S(2)}) copy-start(f32[512]{0:T(512)S(1)} %multiply_reduce_fusion.17) | copy-start | bytes 6148
  69.6 21.1 %copy-start.86 = (f32[512]{0:T(512)}, f32[512]{0:T(512)S(1)}, u32[]{:S(2)}) copy-start(f32[512]{0:T(512)S(1)} %fusion.145) | copy-start | bytes 6148
  70.6 21.7 %copy-start.28 = (bf16[512,128]{0,1:T(8,128)(2,1)}, bf16[512,128]{0,1:T(8,128)(2,1)S(1)}, u32[]{:S(2)}) copy-start(bf16[512,128]{0,1:T(8,128)(2,1)S(1)} %get-tuple-element.144) | copy-start | bytes 393220
  72.4 19.4 %collective-permute-start.7 = (bf16[128,128]{0,1:T(8,128)(2,1)S(1)}, bf16[128,128]{0,1:T(8,128)(2,1)}, u32[]{:S(2)}, u32[]{:S(2)}) collective-permute-start(bf16[128,128]{0,1:T(8,128)(2,1)S(1)} %get-tuple-element.109), channel_id=1, source_target_pairs={{4,0},{8,4},{12,8},{16,12},{20,16},{24,20},{28,24},{5,1},{9,5},{13... | collective-permute-start | bytes 98312 | tf_op jit(solution)/shard_map/ppermute | solution.py:10
  73.7 18.7 %collective-permute-start.6 = (bf16[128,128]{0,1:T(8,128)(2,1)S(1)}, bf16[128,128]{0,1:T(8,128)(2,1)}, u32[]{:S(2)}, u32[]{:S(2)}) collective-permute-start(bf16[128,128]{0,1:T(8,128)(2,1)S(1)} %get-tuple-element.110), channel_id=1, source_target_pairs={{0,4},{4,8},{8,12},{12,16},{16,20},{20,24},{24,28},{1,5},{5,9},{9,... | collective-permute-start | bytes 98312 | tf_op jit(solution)/shard_map/ppermute | solution.py:10
  79.8 12.0 %collective-permute-start.5 = (bf16[64,128]{0,1:T(8,128)(2,1)}, bf16[64,128]{0,1:T(8,128)(2,1)S(1)}, u32[]{:S(2)}, u32[]{:S(2)}) collective-permute-start(bf16[64,128]{0,1:T(8,128)(2,1)} %get-tuple-element.111), channel_id=1, source_target_pairs={{1,0},{2,1},{3,2},{5,4},{6,5},{7,6},{9,8},{10,9},{11,10},{13,12},{... | collective-permute-start | bytes 49160 | tf_op jit(solution)/shard_map/ppermute | solution.py:10
  81.0 10.7 %collective-permute-start.4 = (bf16[64,128]{0,1:T(8,128)(2,1)S(1)}, bf16[64,128]{0,1:T(8,128)(2,1)S(1)}, u32[]{:S(2)}, u32[]{:S(2)}) collective-permute-start(bf16[64,128]{0,1:T(8,128)(2,1)S(1)} %get-tuple-element.112), channel_id=1, source_target_pairs={{0,1},{1,2},{2,3},{4,5},{5,6},{6,7},{8,9},{9,10},{10,11},{12,13},{... | collective-permute-start | bytes 49160 | tf_op jit(solution)/shard_map/ppermute | solution.py:10
  124.6 22.8 %copy-start.15 = (f32[512,128]{0,1:T(8,128)}, f32[512,128]{0,1:T(8,128)S(1)}, u32[]{:S(2)}) copy-start(f32[512,128]{0,1:T(8,128)S(1)} %get-tuple-element.151) | copy-start | bytes 786436
  124.6 23.8 %copy-start.33 = (bf16[512,128]{0,1:T(8,128)(2,1)}, bf16[512,128]{0,1:T(8,128)(2,1)S(1)}, u32[]{:S(2)}) copy-start(bf16[512,128]{0,1:T(8,128)(2,1)S(1)} %get-tuple-element.150) | copy-start | bytes 393220
  127.7 20.8 %collective-permute-start.9 = (bf16[64,128]{0,1:T(8,128)(2,1)}, bf16[64,128]{0,1:T(8,128)(2,1)}, u32[]{:S(2)}, u32[]{:S(2)}) collective-permute-start(bf16[64,128]{0,1:T(8,128)(2,1)} %get-tuple-element.107), channel_id=1, source_target_pairs={{1,0},{2,1},{3,2},{5,4},{6,5},{7,6},{9,8},{10,9},{11,10},{13,12},{... | collective-permute-start | bytes 49160 | tf_op jit(solution)/shard_map/ppermute | solution.py:10
  128.9 19.5 %collective-permute-start.8 = (bf16[64,128]{0,1:T(8,128)(2,1)}, bf16[64,128]{0,1:T(8,128)(2,1)}, u32[]{:S(2)}, u32[]{:S(2)}) collective-permute-start(bf16[64,128]{0,1:T(8,128)(2,1)} %get-tuple-element.108), channel_id=1, source_target_pairs={{0,1},{1,2},{2,3},{4,5},{5,6},{6,7},{8,9},{9,10},{10,11},{12,13},{... | collective-permute-start | bytes 49160 | tf_op jit(solution)/shard_map/ppermute | solution.py:10
  133.4 15.0 %collective-permute-start.11 = (bf16[128,128]{0,1:T(8,128)(2,1)}, bf16[128,128]{0,1:T(8,128)(2,1)}, u32[]{:S(2)}, u32[]{:S(2)}) collective-permute-start(bf16[128,128]{0,1:T(8,128)(2,1)} %get-tuple-element.105), channel_id=1, source_target_pairs={{4,0},{8,4},{12,8},{16,12},{20,16},{24,20},{28,24},{5,1},{9,5},{13... | collective-permute-start | bytes 98312 | tf_op jit(solution)/shard_map/ppermute | solution.py:10
  134.7 13.8 %collective-permute-start.10 = (bf16[128,128]{0,1:T(8,128)(2,1)}, bf16[128,128]{0,1:T(8,128)(2,1)}, u32[]{:S(2)}, u32[]{:S(2)}) collective-permute-start(bf16[128,128]{0,1:T(8,128)(2,1)} %get-tuple-element.106), channel_id=1, source_target_pairs={{0,4},{4,8},{8,12},{12,16},{16,20},{20,24},{24,28},{1,5},{5,9},{9,... | collective-permute-start | bytes 98312 | tf_op jit(solution)/shard_map/ppermute | solution.py:10
  140.1 45.5 %copy-start.5 = (f32[512,128]{0,1:T(8,128)}, f32[512,128]{0,1:T(8,128)S(1)}, u32[]{:S(2)}) copy-start(f32[512,128]{0,1:T(8,128)S(1)} %copy.95) | copy-start | bytes 786436
  213.0 25.3 %copy-start.73 = (s32[2048]{0:T(1024)S(1)}, s32[2048]{0:T(1024)}, u32[]{:S(2)}) copy-start(s32[2048]{0:T(1024)} %get-tuple-element.117) | copy-start | bytes 24580
  228.4 39.3 %collective-permute-start.12 = (bf16[64,128]{1,0:T(8,128)(2,1)}, bf16[64,128]{1,0:T(8,128)(2,1)S(1)}, u32[]{:S(2)}, u32[]{:S(2)}) collective-permute-start(bf16[64,128]{1,0:T(8,128)(2,1)} %get-tuple-element.101), channel_id=1, source_target_pairs={{0,1},{1,2},{2,3},{4,5},{5,6},{6,7},{8,9},{9,10},{10,11},{12,13},{... | collective-permute-start | bytes 49160 | tf_op jit(solution)/shard_map/ppermute | solution.py:10
  231.1 36.5 %collective-permute-start.13 = (bf16[64,128]{1,0:T(8,128)(2,1)}, bf16[64,128]{1,0:T(8,128)(2,1)}, u32[]{:S(2)}, u32[]{:S(2)}) collective-permute-start(bf16[64,128]{1,0:T(8,128)(2,1)} %get-tuple-element.102), channel_id=1, source_target_pairs={{1,0},{2,1},{3,2},{5,4},{6,5},{7,6},{9,8},{10,9},{11,10},{13,12},{... | collective-permute-start | bytes 49160 | tf_op jit(solution)/shard_map/ppermute | solution.py:10
  232.4 35.2 %collective-permute-start.14 = (bf16[128,128]{1,0:T(8,128)(2,1)}, bf16[128,128]{1,0:T(8,128)(2,1)}, u32[]{:S(2)}, u32[]{:S(2)}) collective-permute-start(bf16[128,128]{1,0:T(8,128)(2,1)} %get-tuple-element.103), channel_id=1, source_target_pairs={{0,4},{4,8},{8,12},{12,16},{16,20},{20,24},{24,28},{1,5},{5,9},{9,... | collective-permute-start | bytes 98312 | tf_op jit(solution)/shard_map/ppermute | solution.py:10
  237.0 30.7 %collective-permute-start.15 = (bf16[128,128]{1,0:T(8,128)(2,1)S(1)}, bf16[128,128]{1,0:T(8,128)(2,1)}, u32[]{:S(2)}, u32[]{:S(2)}) collective-permute-start(bf16[128,128]{1,0:T(8,128)(2,1)S(1)} %get-tuple-element.104), channel_id=1, source_target_pairs={{4,0},{8,4},{12,8},{16,12},{20,16},{24,20},{28,24},{5,1},{9,5},{13... | collective-permute-start | bytes 98312 | tf_op jit(solution)/shard_map/ppermute | solution.py:10
  238.3 17.2 %copy-start.70 = (f32[32768]{0:T(1024)S(1)}, f32[32768]{0:T(1024)}, u32[]{:S(2)}) copy-start(f32[32768]{0:T(1024)} %fusion.25) | copy-start | bytes 393220
  238.3 24.2 %copy-start.50 = (f32[16384]{0:T(1024)S(1)}, f32[16384]{0:T(1024)}, u32[]{:S(2)}) copy-start(f32[16384]{0:T(1024)} %fusion.37) | copy-start | bytes 196612
  250.0 21.0 %copy-start.14 = (f32[512,128]{0,1:T(8,128)S(1)}, f32[512,128]{0,1:T(8,128)}, u32[]{:S(2)}) copy-start(f32[512,128]{0,1:T(8,128)} %copy-done.13) | copy-start | bytes 786436
  250.0 21.0 %copy-start.85 = (f32[512]{0:T(512)S(1)}, f32[512]{0:T(512)}, u32[]{:S(2)}) copy-start(f32[512]{0:T(512)} %copy-done.84) | copy-start | bytes 6148
  250.0 21.0 %copy-start.90 = (f32[512]{0:T(512)S(1)}, f32[512]{0:T(512)}, u32[]{:S(2)}) copy-start(f32[512]{0:T(512)} %copy-done.89) | copy-start | bytes 6148
  250.0 21.0 %copy-start.107 = (f32[128]{0:T(128)S(1)}, f32[128]{0:T(128)}, u32[]{:S(2)}) copy-start(f32[128]{0:T(128)} %get-tuple-element.124) | copy-start | bytes 1540
  251.4 20.3 %copy-start.97 = (f32[512]{0:T(512)S(1)}, f32[512]{0:T(512)}, u32[]{:S(2)}) copy-start(f32[512]{0:T(512)} %copy-done.96) | copy-start | bytes 6148
  326.3 31.6 %copy-start.10 = (f32[512,128]{0,1:T(8,128)S(1)}, f32[512,128]{0,1:T(8,128)}, u32[]{:S(2)}) copy-start(f32[512,128]{0,1:T(8,128)} %copy-done.9) | copy-start | bytes 786436
  327.3 27.5 %collective-permute-start.16 = (bf16[64,128]{1,0:T(8,128)(2,1)}, bf16[64,128]{1,0:T(8,128)(2,1)S(1)}, u32[]{:S(2)}, u32[]{:S(2)}) collective-permute-start(bf16[64,128]{1,0:T(8,128)(2,1)} %get-tuple-element.97), channel_id=1, source_target_pairs={{0,1},{1,2},{2,3},{4,5},{5,6},{6,7},{8,9},{9,10},{10,11},{12,13},{... | collective-permute-start | bytes 49160 | tf_op jit(solution)/shard_map/ppermute | solution.py:10
  330.2 24.7 %collective-permute-start.17 = (bf16[64,128]{1,0:T(8,128)(2,1)}, bf16[64,128]{1,0:T(8,128)(2,1)S(1)}, u32[]{:S(2)}, u32[]{:S(2)}) collective-permute-start(bf16[64,128]{1,0:T(8,128)(2,1)} %get-tuple-element.98), channel_id=1, source_target_pairs={{1,0},{2,1},{3,2},{5,4},{6,5},{7,6},{9,8},{10,9},{11,10},{13,12},{... | collective-permute-start | bytes 49160 | tf_op jit(solution)/shard_map/ppermute | solution.py:10
  331.5 23.4 %collective-permute-start.18 = (bf16[128,128]{1,0:T(8,128)(2,1)}, bf16[128,128]{1,0:T(8,128)(2,1)S(1)}, u32[]{:S(2)}, u32[]{:S(2)}) collective-permute-start(bf16[128,128]{1,0:T(8,128)(2,1)} %get-tuple-element.99), channel_id=1, source_target_pairs={{0,4},{4,8},{8,12},{12,16},{16,20},{20,24},{24,28},{1,5},{5,9},{9,... | collective-permute-start | bytes 98312 | tf_op jit(solution)/shard_map/ppermute | solution.py:10
  335.7 19.1 %collective-permute-start.19 = (bf16[128,128]{1,0:T(8,128)(2,1)}, bf16[128,128]{1,0:T(8,128)(2,1)S(1)}, u32[]{:S(2)}, u32[]{:S(2)}) collective-permute-start(bf16[128,128]{1,0:T(8,128)(2,1)} %get-tuple-element.100), channel_id=1, source_target_pairs={{4,0},{8,4},{12,8},{16,12},{20,16},{24,20},{28,24},{5,1},{9,5},{13... | collective-permute-start | bytes 98312 | tf_op jit(solution)/shard_map/ppermute | solution.py:10
  389.9 56.7 %copy-start.12 = (f32[512,128]{0,1:T(8,128)S(1)}, f32[512,128]{0,1:T(8,128)}, u32[]{:S(2)}) copy-start(f32[512,128]{0,1:T(8,128)} %copy-done.11) | copy-start | bytes 786436
  389.9 56.7 %copy-start.16 = (f32[512,128]{0,1:T(8,128)S(1)}, f32[512,128]{0,1:T(8,128)}, u32[]{:S(2)}) copy-start(f32[512,128]{0,1:T(8,128)} %copy-done.15) | copy-start | bytes 786436
  389.9 56.7 %copy-start.25 = (bf16[512,128]{0,1:T(8,128)(2,1)S(1)}, bf16[512,128]{0,1:T(8,128)(2,1)}, u32[]{:S(2)}) copy-start(bf16[512,128]{0,1:T(8,128)(2,1)} %copy.93) | copy-start | bytes 393220
  389.9 56.7 %copy-start.83 = (f32[512]{0:T(512)S(1)}, f32[512]{0:T(512)}, u32[]{:S(2)}) copy-start(f32[512]{0:T(512)} %copy-done.82) | copy-start | bytes 6148
  390.0 56.7 %copy-start.88 = (f32[512]{0:T(512)S(1)}, f32[512]{0:T(512)}, u32[]{:S(2)}) copy-start(f32[512]{0:T(512)} %copy-done.87) | copy-start | bytes 6148
  390.0 56.7 %copy-start.99 = (f32[128]{0:T(128)S(1)}, f32[128]{0:T(128)}, u32[]{:S(2)}) copy-start(f32[128]{0:T(128)} %get-tuple-element.122) | copy-start | bytes 1540
  390.0 162.6 %all-reduce.5.cloned.1.call-start = ((), (), s32[]{:S(2)}) async-start(), calls=%async_computation.1 | async-start | bytes 4218880 | tf_op jit(solution)/shard_map/psum | solution.py:164
  473.5 7.7 %collective-permute-start.20 = (bf16[64,128]{1,0:T(8,128)(2,1)S(1)}, bf16[64,128]{1,0:T(8,128)(2,1)S(1)}, u32[]{:S(2)}, u32[]{:S(2)}) collective-permute-start(bf16[64,128]{1,0:T(8,128)(2,1)S(1)} %get-tuple-element.93), channel_id=1, source_target_pairs={{0,1},{1,2},{2,3},{4,5},{5,6},{6,7},{8,9},{9,10},{10,11},{12,13},{... | collective-permute-start | bytes 49160 | tf_op jit(solution)/shard_map/ppermute | solution.py:10
  475.2 6.1 %collective-permute-start.21 = (bf16[64,128]{1,0:T(8,128)(2,1)S(1)}, bf16[64,128]{1,0:T(8,128)(2,1)S(1)}, u32[]{:S(2)}, u32[]{:S(2)}) collective-permute-start(bf16[64,128]{1,0:T(8,128)(2,1)S(1)} %get-tuple-element.94), channel_id=1, source_target_pairs={{1,0},{2,1},{3,2},{5,4},{6,5},{7,6},{9,8},{10,9},{11,10},{13,12},{... | collective-permute-start | bytes 49160 | tf_op jit(solution)/shard_map/ppermute | solution.py:10
  476.5 5.0 collective-permute-start.22
  479.9 5.8 %collective-permute-start.23 = (bf16[128,128]{1,0:T(8,128)(2,1)S(1)}, bf16[128,128]{1,0:T(8,128)(2,1)S(1)}, u32[]{:S(2)}, u32[]{:S(2)}) collective-permute-start(bf16[128,128]{1,0:T(8,128)(2,1)S(1)} %get-tuple-element.96), channel_id=1, source_target_pairs={{4,0},{8,4},{12,8},{16,12},{20,16},{24,20},{28,24},{5,1},{9,5},{13... | collective-permute-start | bytes 98312 | tf_op jit(solution)/shard_map/ppermute | solution.py:10
  488.6 69.5 %copy-start.52 = (f32[512,128]{1,0:T(8,128)}, f32[512,128]{1,0:T(8,128)S(1)}, u32[]{:S(2)}) copy-start(f32[512,128]{1,0:T(8,128)S(1)} %scatter_custom_fusion.11) | copy-start | bytes 786436
  (102 other events, 439.5 us)
Sparse Core Ops, SparseCore 0:
  390.0 56.5 all-reduce.2
  450.2 102.3 all-reduce.4
